TPU v7x, 32 devices: a whole 2x2x4 slice. The times are simulated.
32 devices in a mesh: row: 16 (over z, x, core), col: 2 (over y).
Axes of the slice: x: 2, y: 2, z: 4, core: 2. Of those that a mesh axis runs over, the one named last changes fastest.
Arguments:
- teacher_hidden: bfloat16 [512, 4608], P('row', 'col'), as said below
- student_hidden: bfloat16 [512, 3584], P('row', 'col'), as said below
- teacher_embed: bfloat16 [16384, 4608], P(('row', 'col')), may hold values from -0.4861359 to 0.4861359
- student_embed: bfloat16 [16384, 3584], P(('row', 'col')), may hold values from -0.5512263 to 0.5512263
Outputs:
- divergence: float32 [512], P(('row', 'col'))
- mean_divergence: float32 [], replicated
Inputs may be any that keep to these rules, and one draw needn't show every extreme that they name: `teacher_hidden`: entries of order one; a few rows may be far larger. `student_hidden`: entries of order one; a few rows may be far larger.
All inputs are finite; a program needn't handle non-finite values.
Results may differ from a plain program's by a relative error of at most 0.0003.
Values may be sent and summed in bfloat16 or wider, within the bound.
A program may use at most 64 MiB of HBM per device.

v0:
```python
import jax
import jax.numpy as jnp
from jax import lax
from jax.sharding import PartitionSpec as P


def block_stats(logit_teacher, logit_student):
    top_teacher = jnp.max(logit_teacher, 1)
    top_student = jnp.max(logit_student, 1)
    weights = jnp.exp(logit_teacher - top_teacher[:, None])
    sum_teacher = jnp.sum(weights, 1)
    cross_term = jnp.sum(weights * (logit_teacher - logit_student), 1)
    sum_student = jnp.sum(jnp.exp(logit_student - top_student[:, None]), 1)
    return (top_teacher, sum_teacher, cross_term, top_student, sum_student)


def per_device(teacher_hidden, student_hidden, teacher_embed, student_embed):
    tokens = teacher_hidden.shape[0] * lax.axis_size("row")
    full_teacher, full_student = (
        lax.all_gather(teacher_hidden, "col", axis=1, tiled=True),
        lax.all_gather(student_hidden, "col", axis=1, tiled=True),
    )
    logit_teacher = jnp.einsum(
        "td,vd->tv",
        lax.all_gather(full_teacher, "row", axis=0, tiled=True),
        teacher_embed,
        preferred_element_type=jnp.float32,
    )
    logit_student = jnp.einsum(
        "td,vd->tv",
        lax.all_gather(full_student, "row", axis=0, tiled=True),
        student_embed,
        preferred_element_type=jnp.float32,
    )
    current = block_stats(logit_teacher, logit_student)
    partial_stats = tuple((fresh_rows for fresh_rows in current))
    top_teacher, sum_teacher, cross_term, top_student, sum_student = partial_stats
    high_teacher, high_student = lax.pmax((top_teacher, top_student), ("row", "col"))
    teacher_scale = jnp.exp(top_teacher - high_teacher)
    student_scale = jnp.exp(top_student - high_student)
    sum_teacher, cross_term, sum_student = lax.psum(
        (sum_teacher * teacher_scale, cross_term * teacher_scale, sum_student * student_scale),
        ("row", "col"),
    )
    top_teacher, top_student = (high_teacher, high_student)
    divergence = (
        cross_term / sum_teacher
        - top_teacher
        - jnp.log(sum_teacher)
        + top_student
        + jnp.log(sum_student)
    )
    mean_divergence = jnp.mean(divergence)
    own_count = tokens // (lax.axis_size("row") * lax.axis_size("col"))
    own_block = lax.axis_index("row") * lax.axis_size("col") + lax.axis_index("col")
    return (lax.dynamic_slice_in_dim(divergence, own_block * own_count, own_count), mean_divergence)


def solution(mesh):
    return jax.shard_map(
        per_device,
        mesh=mesh,
        in_specs=(
            P("row", "col"),
            P("row", "col"),
            P(("row", "col"), None),
            P(("row", "col"), None),
        ),
        out_specs=(P(("row", "col")), P()),
        check_vma=False,
    )
```

profile of v0, /device:TPU:0, one launch (start us, length us, event | category | flops | bytes accessed | tf_op | source)
XLA Modules:
  0.0 213.5 jit_solution(12317152551401748478)
XLA Ops:
  7.2 0.0 all-gather.5.cloned.1.call-start
  7.2 8.6 %all_gather.14 = bf16[32,3584]{1,0:T(8,128)(2,1)} all-gather(bf16[32,1792]{1,0:T(8,128)(2,1)} %param.5), channel_id=1, replica_groups=mesh['row'=16,'col'=2] {'col'}, dimensions={1}, use_global_device_ids=true | all-gather | bytes 344064 | tf_op jit(solution)/shard_map/all_gather | solution.py:21
  15.9 0.0 all-gather.5.cloned.1.call-update
  15.9 0.0 all-gather.3.cloned.1.call-start
  15.9 6.1 %all_gather.12 = bf16[32,4608]{1,0:T(8,128)(2,1)} all-gather(bf16[32,2304]{1,0:T(8,128)(2,1)} %param.4), channel_id=1, replica_groups=mesh['row'=16,'col'=2] {'col'}, dimensions={1}, use_global_device_ids=true | all-gather | bytes 442368 | tf_op jit(solution)/shard_map/all_gather | solution.py:20
  22.1 0.0 all-gather.3.cloned.1.call-update
  22.1 41.9 %all-gather.5.cloned.1.call-done = bf16[512,3584]{1,0:T(8,128)(2,1)} async-done(((bf16[32,3584]{1,0:T(8,128)(2,1)}), bf16[512,3584]{1,0:T(8,128)(2,1)}) %all-gather.5.cloned.1.call-update) | async-done | bytes 3670032 | tf_op jit(solution)/shard_map/all_gather | solution.py:31
  64.0 5.3 %fusion.5 = (f32[512]{0:T(512)S(1)}, f32[512,512]{0,1:T(8,128)S(1)}) fusion(bf16[512,3584]{1,0:T(8,128)(2,1)} %all-gather.5.cloned.1.call-done, bf16[512,3584]{1,0:T(8,128)(2,1)} %param.7), kind=kOutput, calls=%fused_computation.11 | convolution fusion | flops 1879309824 | bytes 8390656 | tf_op jit(solution)/shard_map/td,vd->tv/dot_general | solution.py:29
  69.2 48.9 %all-gather.3.cloned.1.call-done = bf16[512,4608]{1,0:T(8,128)(2,1)} async-done(((bf16[32,4608]{1,0:T(8,128)(2,1)}), bf16[512,4608]{1,0:T(8,128)(2,1)}) %all-gather.3.cloned.1.call-update) | async-done | bytes 4718608 | tf_op jit(solution)/shard_map/all_gather | solution.py:25
  118.1 5.9 %fusion.4 = (f32[512]{0:T(512)S(1)}, f32[512,512]{0,1:T(8,128)S(1)}) fusion(bf16[512,4608]{1,0:T(8,128)(2,1)} %all-gather.3.cloned.1.call-done, bf16[512,4608]{1,0:T(8,128)(2,1)} %param.6), kind=kOutput, calls=%fused_computation.10 | convolution fusion | flops 2416180736 | bytes 10487808 | tf_op jit(solution)/shard_map/td,vd->tv/dot_general | solution.py:23
  124.0 39.2 %all-reduce.1 = (f32[512]{0:T(512)S(1)}, f32[512]{0:T(512)S(1)}) all-reduce(f32[512]{0:T(512)S(1)} %get-tuple-element.16, f32[512]{0:T(512)S(1)} %get-tuple-element.14), channel_id=1, replica_groups=mesh['row'=16,'col'=2] {'row','col'}, use_global_device_ids=true, to_apply=%region_7.0 | all-reduce | flops 1024 | bytes 8192 | tf_op jit(solution)/shard_map/pmax | solution.py:38
  163.3 0.4 multiply_reduce_fusion
  163.7 40.0 %all-reduce = (f32[512]{0:T(512)S(1)}, f32[512]{0:T(512)S(1)}, f32[512]{0:T(512)S(1)}) all-reduce(f32[512]{0:T(512)S(1)} %get-tuple-element.18, f32[512]{0:T(512)S(1)} %get-tuple-element.13, f32[512]{0:T(512)S(1)} %get-tuple-element.12), channel_id=1, replica_groups=mesh['row'=16,'col'=2] {'row','col'}, use_global_device_ids=true, to_apply=%region_9.0 | all-reduce | flops 1536 | bytes 12288 | tf_op jit(solution)/shard_map/psum | solution.py:41
  203.7 0.6 fusion.3
  204.3 0.6 dynamic_slice.3
  (1 shorter events, 0.0 us)
Async XLA Ops:
  7.2 56.8 %all-gather.5.cloned.1.call-start = ((), (), s32[]{:S(2)}) async-start(), calls=%async_computation.1 | async-start | bytes 3899392 | tf_op jit(solution)/shard_map/all_gather | solution.py:31
  15.9 102.2 %all-gather.3.cloned.1.call-start = ((), (), s32[]{:S(2)}) async-start(), calls=%async_computation | async-start | bytes 5013504 | tf_op jit(solution)/shard_map/all_gather | solution.py:25
Sparse Core Ops, SparseCore 0:
  16.0 47.9 all-gather.4
  66.3 51.8 all-gather.2
where the time goes:
time: 214 us
  blocking collectives  94 us (44%)
  waiting for transfers between devices  90.8 us (42%)
  between operations  15.8 us (7%)
  matrix products  11.2 us (5%)
    all_gather x1, waiting for transfers between devices, per_device(): lax.all_gather(full_teacher, 'row', axis=0, tiled=True)  48.9 us
    all_gather x1, waiting for transfers between devices, per_device(): lax.all_gather(full_student, 'row', axis=0, tiled=True)  41.9 us
    psum x1, blocking collectives, per_device(): lax.psum((sum_teacher * teacher_scale, cross_term * teacher_scale, sum_st...  40 us
    pmax x1, blocking collectives, per_device(): lax.pmax((top_teacher, top_student), ('row', 'col'))  39.2 us
    all_gather x1, blocking collectives, per_device(): lax.all_gather(student_hidden, 'col', axis=1, tiled=True)  8.65 us
    all_gather x1, blocking collectives, per_device(): lax.all_gather(teacher_hidden, 'col', axis=1, tiled=True)  6.13 us
    dot_general x1, matrix products, per_device(): jnp.einsum('td,vd->tv', lax.all_gather(full_teacher, 'row', axis=0, tiled...  5.93 us
    dot_general x1, matrix products, per_device(): jnp.einsum('td,vd->tv', lax.all_gather(full_student, 'row', axis=0, tiled...  5.25 us
  transfers between devices with their start and end apart: 2, of which 2 were waited for; matrix products, arithmetic and copies ran while one was open for 2% of the time, Pallas kernels for 0%

commit v1 on v0

v1 whole, which is shorter than its diff:
```python
import functools
import jax
import jax.numpy as jnp
from jax import lax
from jax.experimental import pallas as pl
from jax.experimental.pallas import tpu as pltpu
from jax.sharding import PartitionSpec as P

MESH = pl.DeviceIdType.MESH
CORES = 2
SIDE = 2
WIDTH = 256
ORDERS = ("xzy", "zyx", "zxy", "yzx", "zxy", "zyx", "zxy", "zyx")
AHEAD = 6
LAGS = (0, 1, 3, 4)


def whole_stats(logit_teacher, logit_student):
    top_teacher = jnp.max(logit_teacher, 0, keepdims=True)
    top_student = jnp.max(logit_student, 0, keepdims=True)
    weights = jnp.exp(logit_teacher - top_teacher)
    sum_teacher = jnp.sum(weights, 0, keepdims=True)
    cross_term = jnp.sum(weights * (logit_teacher - logit_student), 0, keepdims=True)
    sum_student = jnp.sum(jnp.exp(logit_student - top_student), 0, keepdims=True)
    return top_teacher, sum_teacher, cross_term, top_student, sum_student


def merge(parts):
    tops_teacher = [part[0:1, :] for part in parts]
    tops_student = [part[3:4, :] for part in parts]
    top_teacher = functools.reduce(jnp.maximum, tops_teacher)
    top_student = functools.reduce(jnp.maximum, tops_student)
    scale_teacher = [jnp.exp(top - top_teacher) for top in tops_teacher]
    scale_student = [jnp.exp(top - top_student) for top in tops_student]
    sum_teacher = sum(part[1:2, :] * scale for part, scale in zip(parts, scale_teacher))
    cross_term = sum(part[2:3, :] * scale for part, scale in zip(parts, scale_teacher))
    sum_student = sum(part[4:5, :] * scale for part, scale in zip(parts, scale_student))
    return top_teacher, sum_teacher, cross_term, top_student, sum_student


def kernel(depth, n_col, teacher_hidden, student_hidden, teacher_embed, student_embed, out, states,
           teacher_table, student_table, logits, plane, line, own_sem, table_sem,
           send_sem, recv_sem, core_send, core_recv, stat_send, stat_recv):
    row, y = lax.axis_index("row"), lax.axis_index("col")
    z, x, c = row // (SIDE * CORES), (row // CORES) % SIDE, row % CORES
    sizes = {"z": depth, "x": SIDE, "y": n_col}
    here = {"z": z, "x": x, "y": y}
    n_teacher = teacher_hidden.shape[1] // WIDTH
    n_student = student_hidden.shape[1] // WIDTH
    chunks = n_teacher + n_student
    tokens = logits.shape[2]

    own_copies = []
    for k in range(chunks):
        source, first = (teacher_hidden, k) if k < n_teacher else (student_hidden, k - n_teacher)
        copy = pltpu.make_async_copy(
            source.at[:, pl.ds(first * WIDTH, WIDTH)], states.at[k, y, z, x, c], own_sem.at[k]
        )
        copy.start()
        own_copies.append(copy)
    tables = [
        pltpu.make_async_copy(teacher_embed, teacher_table, table_sem.at[0]),
        pltpu.make_async_copy(student_embed, student_table, table_sem.at[1]),
    ]
    for copy in tables:
        copy.start()

    def device(z=z, x=x, c=c, y=y):
        return ((z * SIDE + x) * CORES + c, y)

    group = SIDE * CORES * n_col
    spot = (x * CORES + c) * n_col + y

    def in_plane(place):
        place = lax.rem(place, group)
        return device(x=place // (CORES * n_col), c=(place // n_col) % CORES, y=place % n_col)

    def on_axis(axis, step):
        return {axis: lax.rem(here[axis] + step, sizes[axis])}

    barrier = pltpu.get_barrier_semaphore()
    for step in range(1, group):
        pl.semaphore_signal(barrier, inc=1, device_id=in_plane(spot + step), device_id_type=MESH)
    for step in range(1, depth):
        pl.semaphore_signal(
            barrier, inc=1, device_id=device(**on_axis("z", step)), device_id_type=MESH
        )
    pl.semaphore_wait(barrier, group + depth - 2)

    started = []

    def region(k, done, at):
        index = [slice(None) if axis in done else at[axis] for axis in "yzx"]
        return states.at[(k, *index, c)]

    def base(order, phase):
        return sum(sizes[axis] - 1 for axis in order[:phase])

    def send(k, phase):
        order = ORDERS[k % len(ORDERS)]
        axis, done = order[phase], order[:phase]
        for step in range(1, sizes[axis]):
            slot = base(order, phase) + step - 1
            block = region(k, done, here)
            copy = pltpu.make_async_remote_copy(
                src_ref=block, dst_ref=block, send_sem=send_sem.at[k, slot],
                recv_sem=recv_sem.at[k, slot], device_id=device(**on_axis(axis, step)),
                device_id_type=MESH,
            )
            copy.start()
            started.append(copy)

    def receive(k, phase):
        order = ORDERS[k % len(ORDERS)]
        axis, done = order[phase], order[:phase]
        for step in range(1, sizes[axis]):
            slot = base(order, phase) + step - 1
            source = dict(here)
            source[axis] = lax.rem(here[axis] - step + sizes[axis], sizes[axis])
            block = region(k, done, source)
            pltpu.make_async_remote_copy(
                src_ref=block, dst_ref=block, send_sem=send_sem.at[k, slot],
                recv_sem=recv_sem.at[k, slot], device_id=device(), device_id_type=MESH,
            ).wait_recv()

    def hand_over(k):
        block = states.at[k, :, :, :, c]
        copy = pltpu.make_async_remote_copy(
            src_ref=block, dst_ref=block, send_sem=core_send.at[k], recv_sem=core_recv.at[k],
            device_id=device(c=1 - c), device_id_type=MESH,
        )
        copy.start()
        started.append(copy)

    def take_over(k):
        block = states.at[k, :, :, :, 1 - c]
        pltpu.make_async_remote_copy(
            src_ref=block, dst_ref=block, send_sem=core_send.at[k], recv_sem=core_recv.at[k],
            device_id=device(), device_id_type=MESH,
        ).wait_recv()

    def multiply(k):
        model, first, table = (
            (0, k, teacher_table) if k < n_teacher else (1, k - n_teacher, student_table)
        )
        if first == 0:
            tables[model].wait()
        share = table.shape[1] // n_col
        weights = jnp.concatenate(
            [table[:, j * share + first * WIDTH : j * share + (first + 1) * WIDTH] for j in range(n_col)], 1
        )
        hidden = jnp.concatenate(
            [states[k, j].reshape(tokens, WIDTH) for j in range(n_col)], 1
        )
        product = lax.dot_general(
            weights, hidden, (((1,), (1,)), ((), ())), preferred_element_type=jnp.float32
        )
        if first == 0:
            logits[model] = product
        else:
            logits[model] += product

    for k in range(min(AHEAD, chunks)):
        own_copies[k].wait()
        send(k, 0)
    for tick in range(chunks + LAGS[3]):
        k = tick + AHEAD
        if k < chunks:
            own_copies[k].wait()
            send(k, 0)
        k = tick - LAGS[0]
        if 0 <= k < chunks:
            receive(k, 0)
            send(k, 1)
        k = tick - LAGS[1]
        if 0 <= k < chunks:
            receive(k, 1)
            send(k, 2)
        k = tick - LAGS[2]
        if 0 <= k < chunks:
            receive(k, 2)
            hand_over(k)
        k = tick - LAGS[3]
        if 0 <= k < chunks:
            take_over(k)
            multiply(k)

    def token_block(j, carry):
        columns = pl.ds(pl.multiple_of(j * 128, 128), 128)
        stats = whole_stats(logits[0, :, columns], logits[1, :, columns])
        for i, value in enumerate(stats):
            plane[spot, i : i + 1, columns] = value
        return carry

    lax.fori_loop(0, tokens // 128, token_block, 0)

    def exchange(buffer, mine, count, target, first):
        for step in range(1, count):
            copy = pltpu.make_async_remote_copy(
                src_ref=buffer.at[mine], dst_ref=buffer.at[mine],
                send_sem=stat_send.at[first + step], recv_sem=stat_recv.at[first + step],
                device_id=target(step), device_id_type=MESH,
            )
            copy.start()
            started.append(copy)
        for step in range(1, count):
            source = lax.rem(mine - step + count, count)
            pltpu.make_async_remote_copy(
                src_ref=buffer.at[source], dst_ref=buffer.at[source],
                send_sem=stat_send.at[first + step], recv_sem=stat_recv.at[first + step],
                device_id=device(), device_id_type=MESH,
            ).wait_recv()

    exchange(plane, spot, group, lambda step: in_plane(spot + step), 0)
    for i, value in enumerate(merge([plane.at[j] for j in range(group)])):
        line[z, i : i + 1, :] = value
    exchange(line, z, depth, lambda step: device(**on_axis("z", step)), group)
    top_teacher, sum_teacher, cross_term, top_student, sum_student = merge(
        [line.at[j] for j in range(depth)]
    )
    divergence = (
        cross_term / sum_teacher - top_teacher - jnp.log(sum_teacher)
        + top_student + jnp.log(sum_student)
    )
    out[0:1, :] = divergence
    out[1:2, :] = jnp.broadcast_to(jnp.mean(divergence, axis=1, keepdims=True), (1, tokens))
    for copy in started:
        copy.wait_send()


def fused(teacher_hidden, student_hidden, teacher_embed, student_embed):
    n_row, n_col = lax.axis_size("row"), lax.axis_size("col")
    depth = n_row // (SIDE * CORES)
    block = teacher_hidden.shape[0]
    tokens = block * n_row
    chunks = (teacher_hidden.shape[1] + student_hidden.shape[1]) // WIDTH
    vocab = teacher_embed.shape[0]
    group = SIDE * CORES * n_col
    hops = depth + SIDE + n_col - 3
    dma = pltpu.SemaphoreType.DMA
    out = pl.pallas_call(
        functools.partial(kernel, depth, n_col),
        out_shape=jax.ShapeDtypeStruct((2, tokens), jnp.float32),
        in_specs=[pl.BlockSpec(memory_space=pl.ANY)] * 4,
        out_specs=pl.BlockSpec(memory_space=pltpu.VMEM),
        scratch_shapes=[
            pltpu.VMEM((chunks, n_col, depth, SIDE, CORES, block, WIDTH), jnp.bfloat16),
            pltpu.VMEM(teacher_embed.shape, jnp.bfloat16),
            pltpu.VMEM(student_embed.shape, jnp.bfloat16),
            pltpu.VMEM((2, vocab, tokens), jnp.float32),
            pltpu.VMEM((group, 8, tokens), jnp.float32),
            pltpu.VMEM((depth, 8, tokens), jnp.float32),
            dma((chunks,)),
            dma((2,)),
            dma((chunks, hops)),
            dma((chunks, hops)),
            dma((chunks,)),
            dma((chunks,)),
            dma((group + depth,)),
            dma((group + depth,)),
        ],
        compiler_params=pltpu.CompilerParams(
            collective_id=0, has_side_effects=True, vmem_limit_bytes=60 * 2**20
        ),
    )(teacher_hidden, student_hidden, teacher_embed, student_embed)
    own_count = tokens // (n_row * n_col)
    own_block = lax.axis_index("row") * n_col + lax.axis_index("col")
    return lax.dynamic_slice_in_dim(out[0], own_block * own_count, own_count), out[1, 0]


def block_stats(logit_teacher, logit_student):
    return tuple(value[:, 0] for value in whole_stats_rows(logit_teacher, logit_student))


def whole_stats_rows(logit_teacher, logit_student):
    return tuple(value.T for value in whole_stats(logit_teacher.T, logit_student.T))


def gathered(teacher_hidden, student_hidden, teacher_embed, student_embed):
    tokens = teacher_hidden.shape[0] * lax.axis_size("row")
    logit_teacher, logit_student = (
        jnp.einsum(
            "td,vd->tv",
            lax.all_gather(lax.all_gather(hidden, "col", axis=1, tiled=True), "row", axis=0, tiled=True),
            embed,
            preferred_element_type=jnp.float32,
        )
        for hidden, embed in ((teacher_hidden, teacher_embed), (student_hidden, student_embed))
    )
    top_teacher, sum_teacher, cross_term, top_student, sum_student = block_stats(
        logit_teacher, logit_student
    )
    high_teacher, high_student = lax.pmax((top_teacher, top_student), ("row", "col"))
    teacher_scale = jnp.exp(top_teacher - high_teacher)
    student_scale = jnp.exp(top_student - high_student)
    sum_teacher, cross_term, sum_student = lax.psum(
        (sum_teacher * teacher_scale, cross_term * teacher_scale, sum_student * student_scale),
        ("row", "col"),
    )
    divergence = (
        cross_term / sum_teacher - high_teacher - jnp.log(sum_teacher)
        + high_student + jnp.log(sum_student)
    )
    own_count = tokens // (lax.axis_size("row") * lax.axis_size("col"))
    own_block = lax.axis_index("row") * lax.axis_size("col") + lax.axis_index("col")
    return (
        lax.dynamic_slice_in_dim(divergence, own_block * own_count, own_count),
        jnp.mean(divergence),
    )


def per_device(teacher_hidden, student_hidden, teacher_embed, student_embed):
    whole = all(hidden.shape[1] % WIDTH == 0 for hidden in (teacher_hidden, student_hidden))
    plan = fused if whole and lax.axis_size("row") % (SIDE * CORES) == 0 else gathered
    return plan(teacher_hidden, student_hidden, teacher_embed, student_embed)


def solution(mesh):
    return jax.shard_map(
        per_device,
        mesh=mesh,
        in_specs=(
            P("row", "col"),
            P("row", "col"),
            P(("row", "col"), None),
            P(("row", "col"), None),
        ),
        out_specs=(P(("row", "col")), P()),
        check_vma=False,
    )
```

time: 214 us -> 75 us (0.35)
  blocking collectives: 94 us -> 0 us
  waiting for transfers between devices: 90.8 us -> 0 us
  Pallas kernels: 0 us -> 71.7 us
  between operations: 15.8 us -> 0.65 us
  matrix products: 11.2 us -> 0 us
    all_gather x2 -> x0, waiting for transfers between devices: 90.8 us -> none  [the longest x1 48.9 us: per_device(): lax.all_gather(full_teacher, 'row', axis=0, tiled=True)]
    pallas_call x0 -> x1, Pallas kernels: none -> 71.7 us  [fused(): pl.pallas_call(functools.partial(kernel, depth, n_col), out_shape=jax.Sha...]
    psum x1 -> x0, blocking collectives: 40 us -> none  [per_device(): lax.psum((sum_teacher * teacher_scale, cross_term * teacher_scale, sum_st...]
    pmax x1 -> x0, blocking collectives: 39.2 us -> none  [per_device(): lax.pmax((top_teacher, top_student), ('row', 'col'))]
    all_gather x2 -> x0, blocking collectives: 14.8 us -> none  [the longest x1 8.65 us: per_device(): lax.all_gather(student_hidden, 'col', axis=1, tiled=True)]
    dot_general x2 -> x0, matrix products: 11.2 us -> none  [the longest x1 5.93 us: per_device(): jnp.einsum('td,vd->tv', lax.all_gather(full_teacher, 'row', axis=0, tiled...]
  transfers between devices with their start and end apart: 2 -> 0, of which waited for: 2 -> 0; matrix products, arithmetic and copies ran while one was open for 2% -> 0% of each run, Pallas kernels for 0% -> 0%
where the time goes in v1:
time: 75 us; the launch traced here: 74.8 us
  Pallas kernels  71.7 us (96%)
  local copies, waits for them, and re-layouts  2.46 us (3%)
    pallas_call x1, Pallas kernels, fused(): pl.pallas_call(functools.partial(kernel, depth, n_col), out_shape=jax.Sha...  71.7 us

profile of v1, /device:TPU:0, one launch (start us, length us, event | category | flops | bytes accessed | tf_op | source)
XLA Modules:
  0.0 74.8 jit_solution(1964572771852291153)
XLA Ops:
  0.6 71.7 %shard_map.59 = f32[2,512]{1,0:T(2,128)} custom-call(bf16[32,2304]{1,0:T(8,128)(2,1)} %teacher_hidden.1, bf16[32,1792]{1,0:T(8,128)(2,1)} %student_hidden.1, bf16[512,4608]{1,0:T(8,128)(2,1)} %teacher_embed.1, bf16[512,3584]{1,0:T(8,128)(2,1)} %student_embed.1), custom_call_target="tpu_custom_call" | custom-call | tf_op jit(solution)/shard_map/pallas_call | solution.py:241
  72.4 1.2 %slice.7 = f32[1,1]{1,0:T(1,128)} slice(f32[2,512]{1,0:T(2,128)} %shard_map.59), slice={[1:2], [0:1]} | slice | bytes 8 | tf_op jit(solution)/shard_map/slice | solution.py:268
  73.6 0.7 slice.6
  74.2 0.6 dynamic-slice_bitcast_fusion

commit v2 on v1

v2 whole, which is shorter than its diff:
```python
import functools
import jax
import jax.numpy as jnp
from jax import lax
from jax.experimental import pallas as pl
from jax.experimental.pallas import tpu as pltpu
from jax.sharding import PartitionSpec as P

MESH = pl.DeviceIdType.MESH
CORES = 2
SIDE = 2
WIDTH = 256
LATE = 2
AHEAD = 6
LAGS = (0, 2, 4, 5)
LANES = 128


def whole_stats(logit_teacher, logit_student):
    top_teacher = jnp.max(logit_teacher, 0, keepdims=True)
    top_student = jnp.max(logit_student, 0, keepdims=True)
    weights = jnp.exp(logit_teacher - top_teacher)
    sum_teacher = jnp.sum(weights, 0, keepdims=True)
    cross_term = jnp.sum(weights * (logit_teacher - logit_student), 0, keepdims=True)
    sum_student = jnp.sum(jnp.exp(logit_student - top_student), 0, keepdims=True)
    return top_teacher, sum_teacher, cross_term, top_student, sum_student


def merge_tops(parts, top_row, sum_row, blocks):
    tops = [part[top_row * blocks : (top_row + 1) * blocks, :] for part in parts]
    sums = [part[sum_row * blocks : (sum_row + 1) * blocks, :] for part in parts]
    top = functools.reduce(jnp.maximum, tops)
    return top, sum(value * jnp.exp(old - top) for value, old in zip(sums, tops))


def kernel(depth, n_col, teacher_hidden, student_hidden, teacher_embed, student_embed, out, out_mean,
           states, teacher_table, student_table, logits, weights, totals, plane_t, line_t, plane_s,
           line_s, own_sem, table_sem, send_sem, recv_sem, core_send, core_recv, stat_send, stat_recv):
    row, y = lax.axis_index("row"), lax.axis_index("col")
    z, x, c = row // (SIDE * CORES), (row // CORES) % SIDE, row % CORES
    sizes = {"z": depth, "x": SIDE, "y": n_col}
    here = {"z": z, "x": x, "y": y}
    n_teacher = teacher_hidden.shape[1] // WIDTH
    n_student = student_hidden.shape[1] // WIDTH
    chunks = n_teacher + n_student
    tokens = logits.shape[2]
    blocks = tokens // LANES

    own_copies = []
    for k in range(chunks):
        source, first = (teacher_hidden, k) if k < n_teacher else (student_hidden, k - n_teacher)
        own_copies.append(pltpu.make_async_copy(
            source.at[:, pl.ds(first * WIDTH, WIDTH)], states.at[k, y, z, x, c], own_sem.at[k]
        ))
    late = list(range(chunks - LATE, chunks))
    early = list(range(chunks - LATE))
    for k in late + early:
        own_copies[k].start()
    tables = [
        pltpu.make_async_copy(teacher_embed, teacher_table, table_sem.at[0]),
        pltpu.make_async_copy(student_embed, student_table, table_sem.at[1]),
    ]
    for copy in tables:
        copy.start()

    def device(z=z, x=x, c=c, y=y):
        return ((z * SIDE + x) * CORES + c, y)

    group = SIDE * CORES * n_col
    spot = (x * CORES + c) * n_col + y

    def in_plane(place):
        place = lax.rem(place, group)
        return device(x=place // (CORES * n_col), c=(place // n_col) % CORES, y=place % n_col)

    def shifted(axis, step):
        return lax.rem(here[axis] + step + sizes[axis], sizes[axis])

    barrier = pltpu.get_barrier_semaphore()
    for step in range(1, group):
        pl.semaphore_signal(barrier, inc=1, device_id=in_plane(spot + step), device_id_type=MESH)
    for step in range(1, depth):
        pl.semaphore_signal(
            barrier, inc=1, device_id=device(z=shifted("z", step)), device_id_type=MESH
        )
    pl.semaphore_wait(barrier, group + depth - 2)

    started = []
    everything = slice(None)

    def own(at):
        return at["y"], at["z"], at["x"]

    def z_line(at):
        return at["y"], everything, at["x"]

    def square(at):
        return everything, at["z"], everything

    def by_x(picked, *lanes):
        return lambda at: (at["y"], picked(at), 1 - at["x"], *lanes)

    def by_y(step, picked, *lanes):
        return lambda at: (lax.rem(at["y"] + n_col - step, n_col), picked(at), at["x"], *lanes)

    along_z = [("z", step) for step in range(1, depth)]
    across = [("x", 1)] + [("y", step) for step in range(1, n_col)]
    low = lambda at: slice(0, depth // 2)
    high = lambda at: slice(depth // 2, depth)
    same = lambda at: at["z"]
    rows_all = slice(None)
    left, right = (rows_all, slice(0, WIDTH // 2)), (rows_all, slice(WIDTH // 2, WIDTH))
    others = range(1, n_col)
    plan_early = (
        [(*hop, own) for hop in along_z],
        [(*hop, z_line) for hop in across],
        [("y", step, by_x(low)) for step in others] + [("x", 1, by_y(step, high)) for step in others],
    )
    plan_late = (
        [(*hop, own) for hop in across],
        [("y", step, by_x(same, *left)) for step in others]
        + [("x", 1, by_y(step, same, *right)) for step in others],
        [(*hop, square) for hop in along_z],
    )

    def transfers(k, phase):
        plan = plan_late if k in late else plan_early
        slot = sum(len(part) for part in plan[:phase])
        return [(slot + i, *entry) for i, entry in enumerate(plan[phase])]

    def remote(k, slot, index, target):
        block = states.at[(k, *index[:3], c, *index[3:])]
        return pltpu.make_async_remote_copy(
            src_ref=block, dst_ref=block, send_sem=send_sem.at[k, slot],
            recv_sem=recv_sem.at[k, slot], device_id=target, device_id_type=MESH,
        )

    def send(k, phase):
        if phase == 0:
            own_copies[k].wait()
        for slot, axis, step, index in transfers(k, phase):
            copy = remote(k, slot, index(here), device(**{axis: shifted(axis, step)}))
            copy.start()
            started.append(copy)

    def receive(k, phase):
        for slot, axis, step, index in transfers(k, phase):
            remote(k, slot, index({**here, axis: shifted(axis, -step)}), device()).wait_recv()

    def core_copy(k, of, target):
        block = states.at[k, :, :, :, of]
        return pltpu.make_async_remote_copy(
            src_ref=block, dst_ref=block, send_sem=core_send.at[k], recv_sem=core_recv.at[k],
            device_id=target, device_id_type=MESH,
        )

    def hand_over(k):
        copy = core_copy(k, c, device(c=1 - c))
        copy.start()
        started.append(copy)

    def multiply(k):
        core_copy(k, 1 - c, device()).wait_recv()
        model, first, table = (
            (0, k, teacher_table) if k < n_teacher else (1, k - n_teacher, student_table)
        )
        if first == 0:
            tables[model].wait()
        share = table.shape[1] // n_col
        columns = jnp.concatenate(
            [table[:, j * share + first * WIDTH : j * share + (first + 1) * WIDTH] for j in range(n_col)], 1
        )
        hidden = jnp.concatenate([states[k, j].reshape(tokens, WIDTH) for j in range(n_col)], 1)
        product = lax.dot_general(
            columns, hidden, (((1,), (1,)), ((), ())), preferred_element_type=jnp.float32
        )
        if first == 0:
            logits[model] = product
        else:
            logits[model] += product

    def stat_copy(buffer, place, sem, target):
        return pltpu.make_async_remote_copy(
            src_ref=buffer.at[place], dst_ref=buffer.at[place], send_sem=stat_send.at[sem],
            recv_sem=stat_recv.at[sem], device_id=target, device_id_type=MESH,
        )

    def give_stats(buffer, mine, count, target, base):
        for step in range(1, count):
            copy = stat_copy(buffer, mine, base + step, target(step))
            copy.start()
            started.append(copy)

    def take_stats(buffer, mine, count, base):
        for step in range(1, count):
            source = lax.rem(mine - step + count, count)
            stat_copy(buffer, source, base + step, device()).wait_recv()

    def to_plane(step):
        return in_plane(spot + step)

    def to_line(step):
        return device(z=shifted("z", step))

    def lanes_of(j):
        return pl.ds(pl.multiple_of(j * LANES, LANES), LANES)

    def teacher_local():
        def token_block(j, carry):
            values = logits[0, :, lanes_of(j)]
            top = jnp.max(values, 0, keepdims=True)
            plane_t[spot, pl.ds(j, 1), :] = top
            plane_t[spot, pl.ds(blocks + j, 1), :] = jnp.sum(jnp.exp(values - top), 0, keepdims=True)
            return carry

        lax.fori_loop(0, blocks, token_block, 0)
        give_stats(plane_t, spot, group, to_plane, 0)

    def teacher_plane():
        take_stats(plane_t, spot, group, 0)
        top, total = merge_tops([plane_t.at[j] for j in range(group)], 0, 1, blocks)
        line_t[z, 0:blocks, :] = top
        line_t[z, blocks : 2 * blocks, :] = total
        give_stats(line_t, z, depth, to_line, group)

    def teacher_line():
        take_stats(line_t, z, depth, group)
        top, total = merge_tops([line_t.at[j] for j in range(depth)], 0, 1, blocks)
        totals[0:blocks, :] = top
        totals[blocks : 2 * blocks, :] = total

        def token_block(j, carry):
            weights[:, lanes_of(j)] = jnp.exp(logits[0, :, lanes_of(j)] - totals[pl.ds(j, 1), :])
            return carry

        lax.fori_loop(0, blocks, token_block, 0)

    agenda = {n_teacher - 1: teacher_local, n_teacher + 1: teacher_plane, n_teacher + 3: teacher_line}

    def finish(k):
        multiply(k)
        if k in agenda:
            agenda[k]()

    for k in late:
        send(k, 0)
    for k in early[:AHEAD]:
        send(k, 0)
    for tick in range(len(early) + LAGS[3]):
        if 0 <= tick + AHEAD < len(early):
            send(early[tick + AHEAD], 0)
        if tick - LAGS[0] in early:
            receive(tick - LAGS[0], 0)
            send(tick - LAGS[0], 1)
        if tick - LAGS[1] in early:
            receive(tick - LAGS[1], 1)
            send(tick - LAGS[1], 2)
        if tick == 0:
            for k in late:
                receive(k, 0)
                send(k, 1)
        if tick == max(len(early) - AHEAD, 1):
            for k in late:
                receive(k, 1)
                send(k, 2)
        if tick - LAGS[2] in early:
            receive(tick - LAGS[2], 2)
            hand_over(tick - LAGS[2])
        if tick - LAGS[3] in early:
            finish(tick - LAGS[3])
    for k in late:
        receive(k, 2)
        hand_over(k)
    for k in late:
        finish(k)

    def token_block(j, carry):
        student = logits[1, :, lanes_of(j)]
        gap = logits[0, :, lanes_of(j)] - student
        top = jnp.max(student, 0, keepdims=True)
        plane_s[spot, pl.ds(j, 1), :] = top
        plane_s[spot, pl.ds(blocks + j, 1), :] = jnp.sum(jnp.exp(student - top), 0, keepdims=True)
        plane_s[spot, pl.ds(2 * blocks + j, 1), :] = jnp.sum(
            weights[:, lanes_of(j)] * gap, 0, keepdims=True
        )
        return carry

    lax.fori_loop(0, blocks, token_block, 0)

    def merge_student(parts):
        top, total = merge_tops(parts, 0, 1, blocks)
        return top, total, sum(part[2 * blocks : 3 * blocks, :] for part in parts)

    base = group + depth
    give_stats(plane_s, spot, group, to_plane, base)
    take_stats(plane_s, spot, group, base)
    for i, value in enumerate(merge_student([plane_s.at[j] for j in range(group)])):
        line_s[z, i * blocks : (i + 1) * blocks, :] = value
    give_stats(line_s, z, depth, to_line, base + group)
    take_stats(line_s, z, depth, base + group)
    top_student, sum_student, cross_term = merge_student([line_s.at[j] for j in range(depth)])
    top_teacher, sum_teacher = totals[0:blocks, :], totals[blocks : 2 * blocks, :]
    divergence = (
        cross_term / sum_teacher - top_teacher - jnp.log(sum_teacher)
        + top_student + jnp.log(sum_student)
    )
    out_mean[...] = jnp.sum(jnp.sum(divergence, 1, keepdims=True), 0, keepdims=True) / tokens
    count = out.shape[1]
    mine = row * n_col + y
    per_block = LANES // count
    own_row = lax.broadcasted_iota(jnp.int32, divergence.shape, 0) == mine // per_block
    own_line = jnp.sum(jnp.where(own_row, divergence, 0.0), 0, keepdims=True)
    result = own_line[:, 0:count]
    for i in range(1, per_block):
        here_it_is = lax.rem(mine, per_block) == i
        result = jnp.where(here_it_is, own_line[:, i * count : (i + 1) * count], result)
    out[...] = result
    for copy in started:
        copy.wait_send()


def fused(teacher_hidden, student_hidden, teacher_embed, student_embed):
    n_row, n_col = lax.axis_size("row"), lax.axis_size("col")
    depth = n_row // (SIDE * CORES)
    block = teacher_hidden.shape[0]
    tokens = block * n_row
    own_count = tokens // (n_row * n_col)
    chunks = (teacher_hidden.shape[1] + student_hidden.shape[1]) // WIDTH
    vocab = teacher_embed.shape[0]
    group = SIDE * CORES * n_col
    hops = depth + 3 * (n_col - 1)
    stats = 2 * (group + depth)
    blocks = tokens // LANES
    whole = -(-2 * blocks // 8) * 8
    tail = -(-3 * blocks // 8) * 8
    dma = pltpu.SemaphoreType.DMA
    divergence, mean_divergence = pl.pallas_call(
        functools.partial(kernel, depth, n_col),
        out_shape=(
            jax.ShapeDtypeStruct((1, own_count), jnp.float32),
            jax.ShapeDtypeStruct((1, 1), jnp.float32),
        ),
        in_specs=[pl.BlockSpec(memory_space=pl.ANY)] * 4,
        out_specs=(pl.BlockSpec(memory_space=pltpu.VMEM), pl.BlockSpec(memory_space=pltpu.VMEM)),
        scratch_shapes=[
            pltpu.VMEM((chunks, n_col, depth, SIDE, CORES, block, WIDTH), jnp.bfloat16),
            pltpu.VMEM(teacher_embed.shape, jnp.bfloat16),
            pltpu.VMEM(student_embed.shape, jnp.bfloat16),
            pltpu.VMEM((2, vocab, tokens), jnp.float32),
            pltpu.VMEM((vocab, tokens), jnp.float32),
            pltpu.VMEM((whole, LANES), jnp.float32),
            pltpu.VMEM((group, whole, LANES), jnp.float32),
            pltpu.VMEM((depth, whole, LANES), jnp.float32),
            pltpu.VMEM((group, tail, LANES), jnp.float32),
            pltpu.VMEM((depth, tail, LANES), jnp.float32),
            dma((chunks,)),
            dma((2,)),
            dma((chunks, hops)),
            dma((chunks, hops)),
            dma((chunks,)),
            dma((chunks,)),
            dma((stats,)),
            dma((stats,)),
        ],
        compiler_params=pltpu.CompilerParams(
            collective_id=0, has_side_effects=True, vmem_limit_bytes=60 * 2**20
        ),
    )(teacher_hidden, student_hidden, teacher_embed, student_embed)
    return divergence.reshape(own_count), mean_divergence.reshape(())


def block_stats(logit_teacher, logit_student):
    return tuple(value[:, 0] for value in whole_stats_rows(logit_teacher, logit_student))


def whole_stats_rows(logit_teacher, logit_student):
    return tuple(value.T for value in whole_stats(logit_teacher.T, logit_student.T))


def gathered(teacher_hidden, student_hidden, teacher_embed, student_embed):
    tokens = teacher_hidden.shape[0] * lax.axis_size("row")
    logit_teacher, logit_student = (
        jnp.einsum(
            "td,vd->tv",
            lax.all_gather(lax.all_gather(hidden, "col", axis=1, tiled=True), "row", axis=0, tiled=True),
            embed,
            preferred_element_type=jnp.float32,
        )
        for hidden, embed in ((teacher_hidden, teacher_embed), (student_hidden, student_embed))
    )
    top_teacher, sum_teacher, cross_term, top_student, sum_student = block_stats(
        logit_teacher, logit_student
    )
    high_teacher, high_student = lax.pmax((top_teacher, top_student), ("row", "col"))
    teacher_scale = jnp.exp(top_teacher - high_teacher)
    student_scale = jnp.exp(top_student - high_student)
    sum_teacher, cross_term, sum_student = lax.psum(
        (sum_teacher * teacher_scale, cross_term * teacher_scale, sum_student * student_scale),
        ("row", "col"),
    )
    divergence = (
        cross_term / sum_teacher - high_teacher - jnp.log(sum_teacher)
        + high_student + jnp.log(sum_student)
    )
    own_count = tokens // (lax.axis_size("row") * lax.axis_size("col"))
    own_block = lax.axis_index("row") * lax.axis_size("col") + lax.axis_index("col")
    return (
        lax.dynamic_slice_in_dim(divergence, own_block * own_count, own_count),
        jnp.mean(divergence),
    )


def per_device(teacher_hidden, student_hidden, teacher_embed, student_embed):
    n_row, n_col = lax.axis_size("row"), lax.axis_size("col")
    tokens = teacher_hidden.shape[0] * n_row
    own_count = tokens // (n_row * n_col)
    fits = (
        all(hidden.shape[1] % WIDTH == 0 for hidden in (teacher_hidden, student_hidden))
        and student_hidden.shape[1] // WIDTH >= LATE + 2
        and n_row % (2 * SIDE * CORES) == 0
        and n_col > 1
        and tokens % LANES == 0
        and LANES % own_count == 0
    )
    plan = fused if fits else gathered
    return plan(teacher_hidden, student_hidden, teacher_embed, student_embed)


def solution(mesh):
    return jax.shard_map(
        per_device,
        mesh=mesh,
        in_specs=(
            P("row", "col"),
            P("row", "col"),
            P(("row", "col"), None),
            P(("row", "col"), None),
        ),
        out_specs=(P(("row", "col")), P()),
        check_vma=False,
    )
```

time: 75 us -> 63.8 us (0.85)
  Pallas kernels: 71.7 us -> 60.2 us
  between operations: 0.65 us -> 2.4 us
  local copies, waits for them, and re-layouts: 2.46 us -> 1.11 us
    pallas_call x1, Pallas kernels: 71.7 us -> 60.2 us  [fused(): pl.pallas_call(functools.partial(kernel, depth, n_col), out_shape=(jax.Sh...]
    slice x2 -> x0, local copies, waits for them, and re-layouts: 1.88 us -> none  [the longest x1 1.19 us: fused(): out[1, 0]]
    unnamed x0 -> x1, local copies, waits for them, and re-layouts: none -> 1.11 us
where the time goes in v2:
time: 63.8 us; the launch traced here: 63.7 us
  Pallas kernels  60.2 us (94%)
  between operations  2.4 us (4%)
  local copies, waits for them, and re-layouts  1.11 us (2%)
    pallas_call x1, Pallas kernels, fused(): pl.pallas_call(functools.partial(kernel, depth, n_col), out_shape=(jax.Sh...  60.2 us

profile of v2, /device:TPU:0, one launch (start us, length us, event | category | flops | bytes accessed | tf_op | source)
XLA Modules:
  0.0 63.7 jit_solution(6193136316151803822)
XLA Ops:
  0.6 60.2 %shard_map.59 = (f32[1,16]{1,0:T(1,128)}, f32[1,1]{1,0:T(1,128)}) custom-call(bf16[32,2304]{1,0:T(8,128)(2,1)} %teacher_hidden.1, bf16[32,1792]{1,0:T(8,128)(2,1)} %student_hidden.1, bf16[512,4608]{1,0:T(8,128)(2,1)} %teacher_embed.1, bf16[512,3584]{1,0:T(8,128)(2,1)} %student_embed.1), custom_call_target="tpu_custom_call" | custom-call | tf_op jit(solution)/shard_map/pallas_call | solution.py:337
  60.8 1.1 %copy.8 = f32[16]{0:T(128)} copy(f32[16]{0:T(128)} %bitcast.2) | data formatting | bytes 128
